TPU v7x, 32 devices: a whole 2x2x4 slice. The times are simulated.
32 devices in a mesh: dp: 8 (over y, x, core), tensor: 4 (over z).
Axes of the slice: x: 2, y: 2, z: 4, core: 2. Of those that a mesh axis runs over, the one named last changes fastest.
Arguments:
- tokens: bfloat16 [8192, 2048], P(('dp', 'tensor')), may hold values from -6 to 6
- norm_attn: bfloat16 [2048], P('dp'), may hold values from 0.5 to 1.5
- w_query: bfloat16 [2048, 2048], P('dp', 'tensor'), may hold values from -0.125 to 0.125
- key_matrix: bfloat16 [2048, 1024], P('dp', 'tensor'), may hold values from -0.125 to 0.125
- value_matrix: bfloat16 [2048, 1024], P('dp', 'tensor'), may hold values from -0.125 to 0.125
- gain_query: bfloat16 [128], P('dp'), may hold values from 0.25 to 1.75
- gain_key: bfloat16 [128], P('dp'), may hold values from 0.25 to 1.75
- w_output: bfloat16 [2048, 2048], P('tensor', 'dp'), may hold values from -0.5 to 0.5
- norm_ffn: bfloat16 [2048], P('dp'), may hold values from 0.5 to 1.5
- w_gate: bfloat16 [2048, 6144], P('dp', 'tensor'), may hold values from -0.125 to 0.125
- w_up: bfloat16 [2048, 6144], P('dp', 'tensor'), may hold values from -0.125 to 0.125
- w_down: bfloat16 [6144, 2048], P('tensor', 'dp'), may hold values from -0.078125 to 0.078125
- cotangent: bfloat16 [8192, 2048], P(('dp', 'tensor')), may hold values from -6 to 6
- lengths: int32 [8], replicated, may hold values from 769 to 1024, as said below
- deal_order: int32 [8], replicated, may hold values from 0 to 7, as said below
Outputs:
- block_out: bfloat16 [8192, 2048], P(('dp', 'tensor'))
- grad_tokens: bfloat16 [8192, 2048], P(('dp', 'tensor'))
- grad_norm_attn: float32 [2048], P('dp')
- grad_query: float32 [2048, 2048], P('dp', 'tensor')
- grad_key: float32 [2048, 1024], P('dp', 'tensor')
- grad_value: float32 [2048, 1024], P('dp', 'tensor')
- grad_gain_query: float32 [128], P('dp')
- grad_gain_key: float32 [128], P('dp')
- grad_output: float32 [2048, 2048], P('tensor', 'dp')
- grad_norm_ffn: float32 [2048], P('dp')
- grad_gate: float32 [2048, 6144], P('dp', 'tensor')
- grad_up: float32 [2048, 6144], P('dp', 'tensor')
- grad_down: float32 [6144, 2048], P('tensor', 'dp')
Inputs may be any that keep to these rules, and one draw needn't show every extreme that they name: Data group g takes sequence deal_order[g]; deal_order is a permutation. `lengths`: one group's sequence fills all 1024 of its rows and another's leaves 256 - 1 rows of padding.
All inputs are finite; a program needn't handle non-finite values.
Results may differ from a plain program's by a relative error of at most 0.023.
Values may be sent and summed in bfloat16 or wider, within the bound.
No kernel may reach another device: no remote copies, remote signals or barrier semaphores. Data moves between devices by JAX's collectives and lax.ppermute only.
A program may use at most 192 MiB of HBM per device.

v0:
```python
import jax
import jax.numpy as jnp
from jax import lax
from jax.sharding import PartitionSpec as P

QUERY_HEADS = 16
KEY_VALUE_HEADS = 8
HEAD_SIZE = 128
norm_eps = 1e-06
rope_base = 1000000.0


def rms_scale(value_vectors):
    return lax.rsqrt(jnp.mean(value_vectors * value_vectors, axis=-1, keepdims=True) + norm_eps)


def rope_tables(position):
    half_dim = HEAD_SIZE // 2
    inverse_freq = rope_base ** (-2.0 * jnp.arange(half_dim, dtype=jnp.float32) / HEAD_SIZE)
    angles = position.astype(jnp.float32)[:, None] * inverse_freq[None, :]
    angles = jnp.concatenate([angles, angles], axis=1)
    return (jnp.cos(angles), jnp.sin(angles))


def rotate_half(value_vectors):
    half_dim = value_vectors.shape[-1] // 2
    return jnp.concatenate([-value_vectors[..., half_dim:], value_vectors[..., :half_dim]], axis=-1)


def rotate_back(value_vectors):
    half_dim = value_vectors.shape[-1] // 2
    return jnp.concatenate([value_vectors[..., half_dim:], -value_vectors[..., :half_dim]], axis=-1)


def group_layout(lengths, deal_order, group_id, count_of_rows):
    slots = jnp.arange(deal_order.shape[0], dtype=jnp.int32)
    seq_taken = jnp.sum(jnp.where(slots == group_id, deal_order, 0))
    seq_len = jnp.sum(jnp.where(slots == seq_taken, lengths, 0))
    row_index = jnp.arange(count_of_rows, dtype=jnp.int32)
    segment = (row_index >= seq_len).astype(jnp.int32)
    seg_start = jnp.where(segment == 0, 0, seq_len)
    return (segment, row_index - seg_start, row_index < seq_len)


def contract_rows(left, right):
    return lax.dot_general(
        left, right, (((0,), (0,)), ((), ())), preferred_element_type=jnp.float32
    )


def times_transpose(left, right):
    return lax.dot_general(
        left, right, (((1,), (1,)), ((), ())), preferred_element_type=jnp.float32
    )


def masked_scores(query_head, key_head, allowed):
    scores = jnp.einsum(
        "qgd,kd->gqk", query_head, key_head, preferred_element_type=jnp.float32
    ) * HEAD_SIZE ** (-0.5)
    return jnp.where(allowed[None], scores, -1e30)


def attend_head(query_head, key_head, value_head, allowed):
    scores = masked_scores(query_head, key_head, allowed)
    top_score = jnp.max(scores, axis=-1, keepdims=True)
    raised = jnp.exp(scores - top_score)
    summed = jnp.sum(raised, axis=-1, keepdims=True)
    attn_probs = (raised / summed).astype(jnp.bfloat16)
    context = jnp.einsum("gqk,kd->qgd", attn_probs, value_head, preferred_element_type=jnp.float32)
    return (context.astype(jnp.bfloat16), top_score[..., 0] + jnp.log(summed[..., 0]))


def attend_back(query_head, key_head, value_head, d_context_head, log_total, allowed):
    scores = masked_scores(query_head, key_head, allowed)
    attn_full = jnp.exp(scores - log_total[..., None])
    attn_probs = attn_full.astype(jnp.bfloat16)
    d_value = jnp.einsum(
        "gqk,qgd->kd", attn_probs, d_context_head, preferred_element_type=jnp.float32
    )
    d_probs = jnp.einsum(
        "qgd,kd->gqk", d_context_head, value_head, preferred_element_type=jnp.float32
    )
    row_dot = jnp.sum(attn_full * d_probs, axis=-1, keepdims=True)
    d_scores = (attn_full * (d_probs - row_dot)).astype(jnp.bfloat16)
    d_query = jnp.einsum(
        "gqk,kd->qgd", d_scores, key_head, preferred_element_type=jnp.float32
    ) * HEAD_SIZE ** (-0.5)
    d_key = jnp.einsum(
        "gqk,qgd->kd", d_scores, query_head, preferred_element_type=jnp.float32
    ) * HEAD_SIZE ** (-0.5)
    return (d_query, d_key, d_value)


def norm_back(d_unit, pre_values, pre_scale, gain_values):
    mixed_terms = gain_values * d_unit
    return pre_scale * mixed_terms - pre_values * pre_scale**3 * jnp.mean(
        mixed_terms * pre_values, axis=-1, keepdims=True
    )


def local(
    tokens,
    norm_attn,
    w_query,
    key_matrix,
    value_matrix,
    gain_query,
    gain_key,
    w_output,
    norm_ffn,
    w_gate,
    w_up,
    w_down,
    cotangent,
    lengths,
    deal_order,
):
    local_rows = tokens.shape[0]
    group_rows = local_rows * lax.axis_size("tensor")
    heads_here = QUERY_HEADS // lax.axis_size("tensor")
    key_value_local = KEY_VALUE_HEADS // lax.axis_size("tensor")
    rows_per_group = QUERY_HEADS // KEY_VALUE_HEADS
    q_width = heads_here * HEAD_SIZE
    kv_width = key_value_local * HEAD_SIZE
    segment, position, live_rows = group_layout(
        lengths, deal_order, lax.axis_index("dp"), group_rows
    )
    row_index = jnp.arange(group_rows, dtype=jnp.int32)
    allowed = (segment[:, None] == segment[None, :]) & (row_index[None, :] <= row_index[:, None])
    own_live = lax.dynamic_slice_in_dim(
        live_rows, lax.axis_index("tensor") * local_rows, local_rows
    ).astype(jnp.float32)[:, None]
    cosine_table, sine_table = rope_tables(position)
    cosine_table = cosine_table[:, None, :]
    sine_table = sine_table[:, None, :]
    full_set = (
        lax.all_gather(norm_attn, "dp", axis=0, tiled=True),
        lax.all_gather(w_query, "dp", axis=0, tiled=True),
        lax.all_gather(key_matrix, "dp", axis=0, tiled=True),
        lax.all_gather(value_matrix, "dp", axis=0, tiled=True),
        lax.all_gather(gain_query, "dp", axis=0, tiled=True),
        lax.all_gather(gain_key, "dp", axis=0, tiled=True),
        lax.all_gather(w_output, "dp", axis=1, tiled=True),
        lax.all_gather(norm_ffn, "dp", axis=0, tiled=True),
        lax.all_gather(w_gate, "dp", axis=0, tiled=True),
        lax.all_gather(w_up, "dp", axis=0, tiled=True),
        lax.all_gather(w_down, "dp", axis=1, tiled=True),
    )
    qkv_weight = jnp.concatenate((full_set[1], full_set[2], full_set[3]), axis=1)
    token_rows = tokens.astype(jnp.float32)
    scale_attn = rms_scale(token_rows)
    attention_normed_input = (token_rows * scale_attn * full_set[0].astype(jnp.float32)).astype(
        jnp.bfloat16
    )
    normed_attn_all = lax.all_gather(attention_normed_input, "tensor", axis=0, tiled=True)
    projected = jnp.dot(normed_attn_all, qkv_weight, preferred_element_type=jnp.float32)
    q_pre = projected[:, :q_width].reshape(group_rows, heads_here, HEAD_SIZE)
    key_before_norm = projected[:, q_width : q_width + kv_width].reshape(
        group_rows, key_value_local, HEAD_SIZE
    )
    value_rows = projected[:, q_width + kv_width :].astype(jnp.bfloat16)
    q_scale = rms_scale(q_pre)
    q_unit = q_pre * q_scale * full_set[4].astype(jnp.float32)
    queries = (q_unit * cosine_table + rotate_half(q_unit) * sine_table).astype(jnp.bfloat16)
    k_scale = rms_scale(key_before_norm)
    k_unit = key_before_norm * k_scale * full_set[5].astype(jnp.float32)
    key_rot = (k_unit * cosine_table + rotate_half(k_unit) * sine_table).astype(jnp.bfloat16)
    query_heads = jnp.moveaxis(
        queries.reshape(group_rows, key_value_local, rows_per_group, HEAD_SIZE), 1, 0
    )
    key_heads = jnp.moveaxis(key_rot, 1, 0)
    value_heads = jnp.moveaxis(value_rows.reshape(group_rows, key_value_local, HEAD_SIZE), 1, 0)
    context_heads, log_total = lax.map(
        lambda head_parts: attend_head(head_parts[0], head_parts[1], head_parts[2], allowed),
        (query_heads, key_heads, value_heads),
    )
    context = jnp.moveaxis(context_heads, 0, 1).reshape(group_rows, q_width)
    hidden = token_rows + lax.psum_scatter(
        jnp.dot(context, full_set[6], preferred_element_type=jnp.float32).astype(jnp.bfloat16),
        "tensor",
        scatter_dimension=0,
        tiled=True,
    ).astype(jnp.float32)
    scale_ffn = rms_scale(hidden)
    normed_ffn = (hidden * scale_ffn * full_set[7].astype(jnp.float32)).astype(jnp.bfloat16)
    normed_ffn_all = lax.all_gather(normed_ffn, "tensor", axis=0, tiled=True)
    gate_proj = jnp.dot(normed_ffn_all, full_set[8], preferred_element_type=jnp.float32)
    up_proj = jnp.dot(normed_ffn_all, full_set[9], preferred_element_type=jnp.float32)
    gate_sig = jax.nn.sigmoid(gate_proj)
    activation = (gate_proj * gate_sig * up_proj).astype(jnp.bfloat16)
    block_rows = hidden + lax.psum_scatter(
        jnp.dot(activation, full_set[10], preferred_element_type=jnp.float32).astype(jnp.bfloat16),
        "tensor",
        scatter_dimension=0,
        tiled=True,
    ).astype(jnp.float32)
    block_out = (block_rows * own_live).astype(jnp.bfloat16)
    back_set = (
        lax.all_gather(norm_attn, "dp", axis=0, tiled=True),
        lax.all_gather(w_query, "dp", axis=0, tiled=True),
        lax.all_gather(key_matrix, "dp", axis=0, tiled=True),
        lax.all_gather(value_matrix, "dp", axis=0, tiled=True),
        lax.all_gather(gain_query, "dp", axis=0, tiled=True),
        lax.all_gather(gain_key, "dp", axis=0, tiled=True),
        lax.all_gather(w_output, "dp", axis=1, tiled=True),
        lax.all_gather(norm_ffn, "dp", axis=0, tiled=True),
        lax.all_gather(w_gate, "dp", axis=0, tiled=True),
        lax.all_gather(w_up, "dp", axis=0, tiled=True),
        lax.all_gather(w_down, "dp", axis=1, tiled=True),
    )
    back_qkv = jnp.concatenate((back_set[1], back_set[2], back_set[3]), axis=1)
    d_rows = cotangent.astype(jnp.float32) * own_live
    d_branch = d_rows.astype(jnp.bfloat16)
    d_branch_all = lax.all_gather(d_branch, "tensor", axis=0, tiled=True)
    d_act = times_transpose(d_branch_all, back_set[10])
    grad_down = contract_rows(activation, d_branch_all)
    d_gate = (d_act * up_proj * gate_sig * (1.0 + gate_proj * (1.0 - gate_sig))).astype(
        jnp.bfloat16
    )
    d_up = (d_act * gate_proj * gate_sig).astype(jnp.bfloat16)
    grad_gate = contract_rows(normed_ffn_all, d_gate)
    grad_up = contract_rows(normed_ffn_all, d_up)
    d_normed_ffn = lax.psum_scatter(
        (times_transpose(d_gate, back_set[8]) + times_transpose(d_up, back_set[9])).astype(
            jnp.bfloat16
        ),
        "tensor",
        scatter_dimension=0,
        tiled=True,
    ).astype(jnp.float32)
    part_norm_ffn = jnp.sum(d_normed_ffn * hidden * scale_ffn, axis=0)
    d_hidden = d_rows + norm_back(d_normed_ffn, hidden, scale_ffn, back_set[7].astype(jnp.float32))
    d_attended = d_hidden.astype(jnp.bfloat16)
    d_attended_all = lax.all_gather(d_attended, "tensor", axis=0, tiled=True)
    d_context = times_transpose(d_attended_all, back_set[6]).astype(jnp.bfloat16)
    grad_output = contract_rows(context, d_attended_all)
    d_context_heads = jnp.moveaxis(
        d_context.reshape(group_rows, key_value_local, rows_per_group, HEAD_SIZE), 1, 0
    )
    d_query_heads, d_key_heads, d_value_heads = lax.map(
        lambda head_parts: attend_back(
            head_parts[0], head_parts[1], head_parts[2], head_parts[3], head_parts[4], allowed
        ),
        (query_heads, key_heads, value_heads, d_context_heads, log_total),
    )
    d_queries = jnp.moveaxis(d_query_heads, 0, 1).reshape(group_rows, heads_here, HEAD_SIZE)
    d_keys = jnp.moveaxis(d_key_heads, 0, 1)
    d_value = jnp.moveaxis(d_value_heads, 0, 1).reshape(group_rows, kv_width)
    du_query = d_queries * cosine_table + rotate_back(d_queries * sine_table)
    part_gain_query = jnp.sum(du_query * q_pre * q_scale, axis=(0, 1))
    d_q_pre = norm_back(du_query, q_pre, q_scale, back_set[4].astype(jnp.float32))
    du_key = d_keys * cosine_table + rotate_back(d_keys * sine_table)
    part_gain_key = jnp.sum(du_key * key_before_norm * k_scale, axis=(0, 1))
    d_k_pre = norm_back(du_key, key_before_norm, k_scale, back_set[5].astype(jnp.float32))
    d_projected = jnp.concatenate(
        (d_q_pre.reshape(group_rows, q_width), d_k_pre.reshape(group_rows, kv_width), d_value),
        axis=1,
    ).astype(jnp.bfloat16)
    grad_qkv = contract_rows(normed_attn_all, d_projected)
    grad_query = grad_qkv[:, :q_width]
    grad_key = grad_qkv[:, q_width : q_width + kv_width]
    grad_value = grad_qkv[:, q_width + kv_width :]
    d_normed_attn = lax.psum_scatter(
        times_transpose(d_projected, back_qkv).astype(jnp.bfloat16),
        "tensor",
        scatter_dimension=0,
        tiled=True,
    ).astype(jnp.float32)
    part_norm_attn = jnp.sum(d_normed_attn * token_rows * scale_attn, axis=0)
    d_tokens = d_hidden + norm_back(
        d_normed_attn, token_rows, scale_attn, back_set[0].astype(jnp.float32)
    )
    gain_parts = lax.psum((part_norm_attn, part_norm_ffn, part_gain_query, part_gain_key), "tensor")
    shards = tuple(
        (
            lax.psum_scatter(
                gain_parts[0].astype(jnp.bfloat16), "dp", scatter_dimension=0, tiled=True
            ).astype(jnp.float32),
            lax.psum_scatter(
                grad_query.astype(jnp.bfloat16), "dp", scatter_dimension=0, tiled=True
            ).astype(jnp.float32),
            lax.psum_scatter(
                grad_key.astype(jnp.bfloat16), "dp", scatter_dimension=0, tiled=True
            ).astype(jnp.float32),
            lax.psum_scatter(
                grad_value.astype(jnp.bfloat16), "dp", scatter_dimension=0, tiled=True
            ).astype(jnp.float32),
            lax.psum_scatter(
                gain_parts[2].astype(jnp.bfloat16), "dp", scatter_dimension=0, tiled=True
            ).astype(jnp.float32),
            lax.psum_scatter(
                gain_parts[3].astype(jnp.bfloat16), "dp", scatter_dimension=0, tiled=True
            ).astype(jnp.float32),
            lax.psum_scatter(
                grad_output.astype(jnp.bfloat16), "dp", scatter_dimension=1, tiled=True
            ).astype(jnp.float32),
            lax.psum_scatter(
                gain_parts[1].astype(jnp.bfloat16), "dp", scatter_dimension=0, tiled=True
            ).astype(jnp.float32),
            lax.psum_scatter(
                grad_gate.astype(jnp.bfloat16), "dp", scatter_dimension=0, tiled=True
            ).astype(jnp.float32),
            lax.psum_scatter(
                grad_up.astype(jnp.bfloat16), "dp", scatter_dimension=0, tiled=True
            ).astype(jnp.float32),
            lax.psum_scatter(
                grad_down.astype(jnp.bfloat16), "dp", scatter_dimension=1, tiled=True
            ).astype(jnp.float32),
        )
    )
    return (block_out, d_tokens.astype(jnp.bfloat16)) + shards


def solution(mesh):
    return jax.shard_map(
        local,
        mesh=mesh,
        in_specs=(
            P(("dp", "tensor"), None),
            P("dp"),
            P("dp", "tensor"),
            P("dp", "tensor"),
            P("dp", "tensor"),
            P("dp"),
            P("dp"),
            P("tensor", "dp"),
            P("dp"),
            P("dp", "tensor"),
            P("dp", "tensor"),
            P("tensor", "dp"),
            P(("dp", "tensor"), None),
            P(),
            P(),
        ),
        out_specs=(
            P(("dp", "tensor"), None),
            P(("dp", "tensor"), None),
            P("dp"),
            P("dp", "tensor"),
            P("dp", "tensor"),
            P("dp", "tensor"),
            P("dp"),
            P("dp"),
            P("tensor", "dp"),
            P("dp"),
            P("dp", "tensor"),
            P("dp", "tensor"),
            P("tensor", "dp"),
        ),
        check_vma=False,
    )
```

profile of v0, /device:TPU:0, one launch (start us, length us, event | category | flops | bytes accessed | tf_op | source)
XLA Modules:
  0.0 1377.7 jit_solution(12239359164739884811)
XLA Ops:
  31.5 13.4 all-reduce.8
  51.2 14.9 %all-gather.18.cloned.1.call-done = bf16[2048,256]{1,0:T(8,128)(2,1)} async-done(((bf16[256,256]{1,0:T(8,128)(2,1)}), bf16[2048,256]{1,0:T(8,128)(2,1)}) %all-gather.18.cloned.1.call-update) | async-done | bytes 1048592 | tf_op jit(solution)/shard_map/all_gather | solution.py:140
  68.4 23.1 %all-gather.20.cloned.1.call-done = bf16[2048,256]{1,0:T(8,128)(2,1)} async-done(((bf16[256,256]{1,0:T(8,128)(2,1)}), bf16[2048,256]{1,0:T(8,128)(2,1)}) %all-gather.20.cloned.1.call-update) | async-done | bytes 1048592 | tf_op jit(solution)/shard_map/all_gather | solution.py:141
  93.9 80.5 %all-gather.14.cloned.1.call-done = bf16[1024,2048]{1,0:T(8,128)(2,1)} async-done(((bf16[256,2048]{1,0:T(8,128)(2,1)}), bf16[1024,2048]{1,0:T(8,128)(2,1)}) %all-gather.14.cloned.1.call-update) | async-done | bytes 4194320 | tf_op jit(solution)/shard_map/all_gather | solution.py:156
  206.1 16.8 %while.28 = (s32[]{:T(128)}, bf16[2,1024,2,128]{1,3,2,0:T(8,128)(2,1)}, f32[2,2,1024]{2,1,0:T(2,128)S(1)}, bf16[2,1024,128]{1,2,0:T(8,128)(2,1)S(1)}, bf16[2,102...) while((s32[]{:T(128)}, ...), condition=%wide.region_8.9_spmd.clone, body=%wide.region_5.8_spmd.clone.sunk | while | flops 1102313472 | bytes 31004760 | solution.py:174
  240.0 65.8 %reduce-scatter.12.cloned.1.call-done = bf16[256,2048]{1,0:T(8,128)(2,1)} async-done(((bf16[1024,2048]{1,0:T(8,128)(2,1)}), bf16[256,2048]{1,0:T(8,128)(2,1)}) %reduce-scatter.12.cloned.1.call-update) | async-done | bytes 1048592 | tf_op jit(solution)/shard_map/reduce_scatter | solution.py:179
  313.6 40.3 %all-gather.26.cloned.1.call-done = bf16[2048,1536]{1,0:T(8,128)(2,1)} async-done(((bf16[256,1536]{1,0:T(8,128)(2,1)}), bf16[2048,1536]{1,0:T(8,128)(2,1)}) %all-gather.26.cloned.1.call-update) | async-done | bytes 6291472 | tf_op jit(solution)/shard_map/all_gather | solution.py:146
  353.9 83.0 %all-gather.24.cloned.1.call-done = bf16[1024,2048]{1,0:T(8,128)(2,1)} async-done(((bf16[256,2048]{1,0:T(8,128)(2,1)}), bf16[1024,2048]{1,0:T(8,128)(2,1)}) %all-gather.24.cloned.1.call-update) | async-done | bytes 4194320 | tf_op jit(solution)/shard_map/all_gather | solution.py:187
  436.9 11.9 fusion.113
  448.8 34.2 %all-gather.28.cloned.1.call-done = bf16[2048,1536]{1,0:T(8,128)(2,1)} async-done(((bf16[256,1536]{1,0:T(8,128)(2,1)}), bf16[2048,1536]{1,0:T(8,128)(2,1)}) %all-gather.28.cloned.1.call-update) | async-done | bytes 6291472 | tf_op jit(solution)/shard_map/all_gather | solution.py:147
  483.0 11.7 fusion.114
  494.7 71.2 %all-gather.32.cloned.1.call-done = bf16[1024,2048]{1,0:T(8,128)(2,1)} async-done(((bf16[256,2048]{1,0:T(8,128)(2,1)}), bf16[1024,2048]{1,0:T(8,128)(2,1)}) %all-gather.32.cloned.1.call-update) | async-done | bytes 4194320 | tf_op jit(solution)/shard_map/all_gather | solution.py:215
  565.9 47.3 %all-gather.30.cloned.1.call-done = bf16[1536,2048]{1,0:T(8,128)(2,1)} async-done(((bf16[1536,256]{1,0:T(8,128)(2,1)}), bf16[1536,2048]{1,0:T(8,128)(2,1)}) %all-gather.30.cloned.1.call-update) | async-done | bytes 6291472 | tf_op jit(solution)/shard_map/all_gather | solution.py:148
  613.2 16.5 %multiply_convert_fusion = (bf16[1024,1536]{1,0:T(8,128)(2,1)}, bf16[1024,1536]{1,0:T(8,128)(2,1)S(1)}, bf16[1024,1536]{1,0:T(8,128)(2,1)}) fusion(f32[1024,1536]{1,0:T(8,128)} %fusion.113, f32[1024,1536]{1,0:T(8,128)} %fusion.114, bf16[1024,2048]{1,0:T(8,128)(2,1)} %all-gather.32.cloned.1.call-done, bf16[1536,2048]{1,0:T(8,128)(2,1)} %all-gather.30.cloned.1.call-done), kind=kOutput, calls=%fused_computation.75 | convolution fusion | flops 6467616768 | bytes 32505856 | tf_op jit(solution)/shard_map/dot_general | solution.py:52
  639.7 10.5 add_convert_fusion
  650.2 11.1 convolution_convert_fusion.3
  661.4 65.7 %reduce-scatter.16.cloned.1.call-done = bf16[256,2048]{1,0:T(8,128)(2,1)} async-done(((bf16[1024,2048]{1,0:T(8,128)(2,1)}), bf16[256,2048]{1,0:T(8,128)(2,1)}) %reduce-scatter.16.cloned.1.call-update) | async-done | bytes 1048592 | tf_op jit(solution)/shard_map/reduce_scatter | solution.py:224
  729.6 77.1 %reduce-scatter.14.cloned.1.call-done = bf16[256,2048]{1,0:T(8,128)(2,1)} async-done(((bf16[1024,2048]{1,0:T(8,128)(2,1)}), bf16[256,2048]{1,0:T(8,128)(2,1)}) %reduce-scatter.14.cloned.1.call-update) | async-done | bytes 1048592 | tf_op jit(solution)/shard_map/reduce_scatter | solution.py:192
  811.8 11.5 convolution_convert_fusion.2
  823.3 11.9 convolution_convert_fusion.1
  838.6 11.3 convolution_convert_fusion
  850.0 43.1 %all-gather.34.cloned.1.call-done = bf16[1024,2048]{1,0:T(8,128)(2,1)} async-done(((bf16[256,2048]{1,0:T(8,128)(2,1)}), bf16[1024,2048]{1,0:T(8,128)(2,1)}) %all-gather.34.cloned.1.call-update) | async-done | bytes 4194320 | tf_op jit(solution)/shard_map/all_gather | solution.py:235
  901.8 27.5 %while.29 = (s32[]{:T(128)}, f32[2,1024,2,128]{1,3,2,0:T(8,128)}, f32[2,1024,128]{2,1,0:T(8,128)}, bf16[2,1024,128]{2,1,0:T(8,128)(2,1)}, bf16[2,1024,128]{2,1,0...) while((s32[]{:T(128)}, f32[2,1024,2,128]{1,3,2,0:T(8,128)}, ...), condition=%wide.region_16.17_spmd.clone, body=%wide.region_14.16_spmd.clone.sunk | while | flops 2719348736 | bytes 101516552 | solution.py:241
  974.8 47.3 %reduce-scatter.30.cloned.1.call-done = bf16[256,1536]{1,0:T(8,128)(2,1)} async-done(((bf16[2048,1536]{1,0:T(8,128)(2,1)}), bf16[256,1536]{1,0:T(8,128)(2,1)}) %reduce-scatter.30.cloned.1.call-update) | async-done | bytes 786448 | tf_op jit(solution)/shard_map/reduce_scatter | solution.py:304
  1024.6 62.9 %reduce-scatter.32.cloned.1.call-done = bf16[1536,256]{1,0:T(8,128)(2,1)} async-done(((bf16[1536,2048]{1,0:T(8,128)(2,1)}), bf16[1536,256]{1,0:T(8,128)(2,1)}) %reduce-scatter.32.cloned.1.call-update) | async-done | bytes 786448 | tf_op jit(solution)/shard_map/reduce_scatter | solution.py:307
  1089.9 36.7 %reduce-scatter.22.cloned.1.call-done = bf16[256,256]{1,0:T(8,128)(2,1)} async-done(((bf16[2048,256]{1,0:T(8,128)(2,1)}), bf16[256,256]{1,0:T(8,128)(2,1)}) %reduce-scatter.22.cloned.1.call-update) | async-done | bytes 131088 | tf_op jit(solution)/shard_map/reduce_scatter | solution.py:283
  1128.2 37.6 %reduce-scatter.24.cloned.1.call-done = bf16[256,256]{1,0:T(8,128)(2,1)} async-done(((bf16[2048,256]{1,0:T(8,128)(2,1)}), bf16[256,256]{1,0:T(8,128)(2,1)}) %reduce-scatter.24.cloned.1.call-update) | async-done | bytes 131088 | tf_op jit(solution)/shard_map/reduce_scatter | solution.py:286
  1167.4 42.8 %reduce-scatter.26.cloned.1.call-done = bf16[512,256]{1,0:T(8,128)(2,1)} async-done(((bf16[512,2048]{1,0:T(8,128)(2,1)}), bf16[512,256]{1,0:T(8,128)(2,1)}) %reduce-scatter.26.cloned.1.call-update) | async-done | bytes 262160 | tf_op jit(solution)/shard_map/reduce_scatter | solution.py:295
  1211.9 43.1 %reduce-scatter.20.cloned.1.call-done = bf16[256,512]{1,0:T(8,128)(2,1)} async-done(((bf16[2048,512]{1,0:T(8,128)(2,1)}), bf16[256,512]{1,0:T(8,128)(2,1)}) %reduce-scatter.20.cloned.1.call-update) | async-done | bytes 262160 | tf_op jit(solution)/shard_map/reduce_scatter | solution.py:280
  1256.9 77.3 %reduce-scatter.18.cloned.1.call-done = bf16[256,2048]{1,0:T(8,128)(2,1)} async-done(((bf16[1024,2048]{1,0:T(8,128)(2,1)}), bf16[256,2048]{1,0:T(8,128)(2,1)}) %reduce-scatter.18.cloned.1.call-update) | async-done | bytes 1048592 | tf_op jit(solution)/shard_map/reduce_scatter | solution.py:264
  1336.0 18.2 %all-reduce.6 = (bf16[2048]{0:T(1024)(128)(2,1)S(1)}, bf16[128]{0:T(256)(128)(2,1)S(1)}, bf16[128]{0:T(256)(128)(2,1)S(1)}, bf16[2048]{0:T(1024)(128)(2,1)S(1)}) all-reduce(f32[2048]{0:T(1024)S(1)} %get-tuple-element.175, f32[128]{0:T(128)S(1)} %bitcast_reduce_fusion, ...), channel_id=1, replica_groups=mesh['dp'=8,'tensor'=4] {'tensor'}, use_global_device_ids=true, to_apply=%region_22.23 | all-reduce | flops 4352 | bytes 26112 | tf_op jit(solution)/shard_map/psum | solution.py:274
  1354.2 12.3 all-reduce.7
  (295 shorter events, 225.8 us)
Async XLA Ops:
  7.2 40.8 %all-gather.16.cloned.1.call-start = ((), (), s32[]{:S(2)}) async-start(), calls=%async_computation.12 | async-start | bytes 2359296 | tf_op jit(solution)/shard_map/all_gather | solution.py:139
  8.0 58.1 %all-gather.18.cloned.1.call-start = ((), (), s32[]{:S(2)}) async-start(), calls=%async_computation.13 | async-start | bytes 1179648 | tf_op jit(solution)/shard_map/all_gather | solution.py:140
  8.7 82.8 %all-gather.20.cloned.1.call-start = ((), (), s32[]{:S(2)}) async-start(), calls=%async_computation.14 | async-start | bytes 1179648 | tf_op jit(solution)/shard_map/all_gather | solution.py:141
  9.5 164.9 %all-gather.14.cloned.1.call-start = ((), (), s32[]{:S(2)}) async-start(), calls=%async_computation.11 | async-start | bytes 5242880 | tf_op jit(solution)/shard_map/all_gather | solution.py:156
  25.7 197.3 %all-gather.22.cloned.1.call-start = ((), (), s32[]{:S(2)}) async-start(), calls=%async_computation.15 | async-start | bytes 2359296 | tf_op jit(solution)/shard_map/all_gather | solution.py:144
  26.3 279.5 %reduce-scatter.12.cloned.1.call-start = ((), (), s32[]{:S(2)}) async-start(), calls=%async_computation.16 | async-start | bytes 5242880 | tf_op jit(solution)/shard_map/reduce_scatter | solution.py:179
  44.9 155.3 %copy-start.45 = (f32[128]{0:T(128)}, f32[128]{0:T(128)S(1)}, u32[]{:S(2)}) copy-start(f32[128]{0:T(128)S(1)} %convert_element_type.188) | copy-start | bytes 1540
  48.0 155.0 %copy-start.43 = (f32[128]{0:T(128)}, f32[128]{0:T(128)S(1)}, u32[]{:S(2)}) copy-start(f32[128]{0:T(128)S(1)} %convert_element_type.191) | copy-start | bytes 1540
  230.3 75.5 %copy-start = (bf16[256,2048]{1,0:T(8,128)(2,1)S(1)}, bf16[256,2048]{1,0:T(8,128)(2,1)}, u32[]{:S(2)}) copy-start(bf16[256,2048]{1,0:T(8,128)(2,1)} %param.19) | copy-start | bytes 3145732
  230.3 81.3 %copy-start.23 = (bf16[256,2048]{1,0:T(8,128)(2,1)S(1)}, bf16[256,2048]{1,0:T(8,128)(2,1)}, u32[]{:S(2)}) copy-start(bf16[256,2048]{1,0:T(8,128)(2,1)} %param.31) | copy-start | bytes 3145732
  230.3 123.6 %all-gather.26.cloned.1.call-start = ((), (), s32[]{:S(2)}) async-start(), calls=%async_computation.18 | async-start | bytes 7077888 | tf_op jit(solution)/shard_map/all_gather | solution.py:146
  231.0 205.9 %all-gather.24.cloned.1.call-start = ((), (), s32[]{:S(2)}) async-start(), calls=%async_computation.17 | async-start | bytes 5242880 | tf_op jit(solution)/shard_map/all_gather | solution.py:187
  310.0 173.0 %all-gather.28.cloned.1.call-start = ((), (), s32[]{:S(2)}) async-start(), calls=%async_computation.19 | async-start | bytes 7077888 | tf_op jit(solution)/shard_map/all_gather | solution.py:147
  310.8 255.1 %all-gather.32.cloned.1.call-start = ((), (), s32[]{:S(2)}) async-start(), calls=%async_computation.22 | async-start | bytes 5242880 | tf_op jit(solution)/shard_map/all_gather | solution.py:215
  312.8 300.3 %all-gather.30.cloned.1.call-start = ((), (), s32[]{:S(2)}) async-start(), calls=%async_computation.20 | async-start | bytes 7077888 | tf_op jit(solution)/shard_map/all_gather | solution.py:148
  313.6 413.5 %reduce-scatter.16.cloned.1.call-start = ((), (), s32[]{:S(2)}) async-start(), calls=%async_computation.23 | async-start | bytes 5242880 | tf_op jit(solution)/shard_map/reduce_scatter | solution.py:224
  650.2 156.5 %reduce-scatter.14.cloned.1.call-start = ((), (), s32[]{:S(2)}) async-start(), calls=%async_computation.21 | async-start | bytes 5242880 | tf_op jit(solution)/shard_map/reduce_scatter | solution.py:192
  661.3 231.8 %all-gather.34.cloned.1.call-start = ((), (), s32[]{:S(2)}) async-start(), calls=%async_computation.24 | async-start | bytes 5242880 | tf_op jit(solution)/shard_map/all_gather | solution.py:235
  811.8 160.4 %reduce-scatter.28.cloned.1.call-start = ((), (), s32[]{:S(2)}) async-start(), calls=%async_computation.30 | async-start | bytes 7077888 | tf_op jit(solution)/shard_map/reduce_scatter | solution.py:301
  823.3 198.8 %reduce-scatter.30.cloned.1.call-start = ((), (), s32[]{:S(2)}) async-start(), calls=%async_computation.31 | async-start | bytes 7077888 | tf_op jit(solution)/shard_map/reduce_scatter | solution.py:304
  835.3 252.2 %reduce-scatter.32.cloned.1.call-start = ((), (), s32[]{:S(2)}) async-start(), calls=%async_computation.32 | async-start | bytes 7077888 | tf_op jit(solution)/shard_map/reduce_scatter | solution.py:307
  850.0 276.6 %reduce-scatter.22.cloned.1.call-start = ((), (), s32[]{:S(2)}) async-start(), calls=%async_computation.27 | async-start | bytes 1179648 | tf_op jit(solution)/shard_map/reduce_scatter | solution.py:283
  952.1 213.6 %reduce-scatter.24.cloned.1.call-start = ((), (), s32[]{:S(2)}) async-start(), calls=%async_computation.28 | async-start | bytes 1179648 | tf_op jit(solution)/shard_map/reduce_scatter | solution.py:286
  952.9 257.2 %reduce-scatter.26.cloned.1.call-start = ((), (), s32[]{:S(2)}) async-start(), calls=%async_computation.29 | async-start | bytes 2359296 | tf_op jit(solution)/shard_map/reduce_scatter | solution.py:295
  959.1 295.9 %reduce-scatter.20.cloned.1.call-start = ((), (), s32[]{:S(2)}) async-start(), calls=%async_computation.26 | async-start | bytes 2359296 | tf_op jit(solution)/shard_map/reduce_scatter | solution.py:280
  962.3 371.8 %reduce-scatter.18.cloned.1.call-start = ((), (), s32[]{:S(2)}) async-start(), calls=%async_computation.25 | async-start | bytes 5242880 | tf_op jit(solution)/shard_map/reduce_scatter | solution.py:264
  972.1 362.0 %copy-start.1 = (bf16[256,2048]{1,0:T(8,128)(2,1)S(1)}, bf16[256,2048]{1,0:T(8,128)(2,1)}, u32[]{:S(2)}) copy-start(bf16[256,2048]{1,0:T(8,128)(2,1)} %param.19) | copy-start | bytes 3145732
  972.1 362.0 %copy-start.37 = (f32[8,1,256]{2,1,0:T(1,128)S(1)}, f32[8,1,256]{2,1,0:T(1,128)}, u32[]{:S(2)}) copy-start(f32[8,1,256]{2,1,0:T(1,128)} %copy-done.36) | copy-start | bytes 24580
  972.1 362.0 %copy-start.42 = (f32[256]{0:T(256)S(1)}, f32[256]{0:T(256)}, u32[]{:S(2)}) copy-start(f32[256]{0:T(256)} %copy-done.41) | copy-start | bytes 3076
  974.8 361.3 %copy-start.40 = (f32[2048]{0:T(1024)S(1)}, f32[2048]{0:T(1024)}, u32[]{:S(2)}) copy-start(f32[2048]{0:T(1024)} %get-tuple-element.171) | copy-start | bytes 24580
  974.8 393.0 %copy-start.17 = (f32[256,2048]{1,0:T(8,128)S(1)}, f32[256,2048]{1,0:T(8,128)}, u32[]{:S(2)}) copy-start(f32[256,2048]{1,0:T(8,128)} %get-tuple-element.223) | copy-start | bytes 6291460
  974.8 393.0 %copy-start.47 = (f32[256]{0:T(256)S(1)}, f32[256]{0:T(256)}, u32[]{:S(2)}) copy-start(f32[256]{0:T(256)} %get-tuple-element.252) | copy-start | bytes 3076
  (53 other events, 368.8 us)
Sparse Core Ops, SparseCore 0:
  10.0 30.6 all-gather.15
  42.5 23.5 all-gather.17
  68.0 23.4 all-gather.19
  93.5 80.7 all-gather.13
  176.0 26.7 all-gather.21
  230.4 75.3 reduce-scatter.11
  307.8 46.0 all-gather.25
  356.1 80.7 all-gather.23
  438.9 44.0 all-gather.27
  485.1 80.7 all-gather.31
  567.9 45.1 all-gather.29
  650.3 76.7 reduce-scatter.15
  729.4 77.2 reduce-scatter.13
  811.9 81.2 all-gather.33
  896.8 60.2 reduce-scatter.27
  960.3 61.7 reduce-scatter.29
  1025.7 61.7 reduce-scatter.31
  1090.5 36.0 reduce-scatter.21
  1129.7 35.9 reduce-scatter.23
  1168.9 41.2 reduce-scatter.25
  1213.8 41.2 reduce-scatter.19
  1257.4 76.7 reduce-scatter.17
where the time goes:
time: 1390 us; the launch traced here: 1380 us
  waiting for transfers between devices  999 us (72%)
  matrix products  176 us (13%)
  other arithmetic  76.1 us (5%)
  blocking collectives  63.1 us (5%)
  local copies, waits for them, and re-layouts  44.2 us (3%)
  between operations  17.3 us (1%)
    all_gather x1, waiting for transfers between devices, local(): normed_ffn_all = lax.all_gather(normed_ffn, 'tensor', axis=0, tiled=True)  83 us
    all_gather x1, waiting for transfers between devices, local(): lax.all_gather(attention_normed_input, 'tensor', axis=0, tiled=True)  80.5 us
    reduce_scatter x1, waiting for transfers between devices, local(): lax.psum_scatter(times_transpose(d_projected, back_qkv).astype(jnp.bfloat...  77.3 us
    reduce_scatter x1, waiting for transfers between devices, local(): lax.psum_scatter(jnp.dot(activation, full_set[10], preferred_element_type...  77.1 us
    all_gather x1, waiting for transfers between devices, local(): d_branch_all = lax.all_gather(d_branch, 'tensor', axis=0, tiled=True)  71.2 us
    reduce_scatter x1, waiting for transfers between devices, local(): lax.psum_scatter(jnp.dot(context, full_set[6], preferred_element_type=jnp...  65.8 us
    reduce_scatter x1, waiting for transfers between devices, local(): lax.psum_scatter((times_transpose(d_gate, back_set[8]) + times_transpose(...  65.7 us
    reduce_scatter x1, waiting for transfers between devices, local(): lax.psum_scatter(grad_down.astype(jnp.bfloat16), 'dp', scatter_dimension=...  62.9 us
  transfers between devices with their start and end apart: 22, of which 19 were waited for; matrix products, arithmetic and copies ran while one was open for 17% of the time, Pallas kernels for 0%

commit v1 on v0

--- a/solution.py
+++ b/solution.py
@@ -8,6 +8,22 @@
 HEAD_SIZE = 128
 norm_eps = 1e-06
 rope_base = 1000000.0
+
+
+def gather_around(x, axis, dim):
+    ways, here, step = (lax.axis_size(axis), lax.axis_index(axis), x.shape[dim])
+    shape = [n * ways if d == dim else n for d, n in enumerate(x.shape)]
+    full = lax.dynamic_update_slice_in_dim(jnp.zeros(shape, x.dtype), x, here * step, axis=dim)
+    going_up = going_down = x
+    for far in range(1, ways // 2 + 1):
+        going_up = lax.ppermute(going_up, axis, [(d, (d + 1) % ways) for d in range(ways)])
+        full = lax.dynamic_update_slice_in_dim(full, going_up, (here - far) % ways * step, axis=dim)
+        if 2 * far < ways:
+            going_down = lax.ppermute(going_down, axis, [(d, (d - 1) % ways) for d in range(ways)])
+            full = lax.dynamic_update_slice_in_dim(
+                full, going_down, (here + far) % ways * step, axis=dim
+            )
+    return full
 
 
 def rms_scale(value_vectors):
@@ -184,7 +200,7 @@
     ).astype(jnp.float32)
     scale_ffn = rms_scale(hidden)
     normed_ffn = (hidden * scale_ffn * full_set[7].astype(jnp.float32)).astype(jnp.bfloat16)
-    normed_ffn_all = lax.all_gather(normed_ffn, "tensor", axis=0, tiled=True)
+    normed_ffn_all = gather_around(normed_ffn, "tensor", 0)
     gate_proj = jnp.dot(normed_ffn_all, full_set[8], preferred_element_type=jnp.float32)
     up_proj = jnp.dot(normed_ffn_all, full_set[9], preferred_element_type=jnp.float32)
     gate_sig = jax.nn.sigmoid(gate_proj)

time: 1390 us -> 1370 us (0.986)
  waiting for transfers between devices: 999 us -> 923 us
  starting transfers between devices: 0.88 us -> 48 us
    all_gather x1 -> x0, waiting for transfers between devices: 83 us -> none  [local(): normed_ffn_all = lax.all_gather(normed_ffn, 'tensor', axis=0, tiled=True)]
    reduce_scatter x1, waiting for transfers between devices: 0.02 us -> 47.3 us  [local(): lax.psum_scatter(grad_gate.astype(jnp.bfloat16), 'dp', scatter_dimension=...]
    reduce_scatter x1, waiting for transfers between devices: 47.3 us -> 0.02 us  [local(): lax.psum_scatter(grad_up.astype(jnp.bfloat16), 'dp', scatter_dimension=0,...]
    ppermute x0 -> x3, starting transfers between devices: none -> 47.2 us  [the longest x2 44.8 us: gather_around(): lax.ppermute(going_up, axis, [(d, (d + 1) % ways) for d in range(ways)])]
    ppermute x0 -> x3, waiting for transfers between devices: none -> 43 us  [the longest x2 43 us: gather_around(): lax.ppermute(going_up, axis, [(d, (d + 1) % ways) for d in range(ways)])]
    all_gather x1, waiting for transfers between devices: 71.2 us -> 49.4 us  [local(): d_branch_all = lax.all_gather(d_branch, 'tensor', axis=0, tiled=True)]
  transfers between devices with their start and end apart: 22 -> 24, of which waited for: 19 -> 19; matrix products, arithmetic and copies ran while one was open for 17% -> 18% of each run, Pallas kernels for 0% -> 0%
where the time goes in v1:
time: 1370 us; the launch traced here: 1360 us
  waiting for transfers between devices  923 us (67%)
  matrix products  176 us (13%)
  other arithmetic  75.4 us (6%)
  blocking collectives  63.1 us (5%)
  local copies, waits for them, and re-layouts  53 us (4%)
  starting transfers between devices  48 us (4%)
  between operations  17.3 us (1%)
    all_gather x1, waiting for transfers between devices, local(): lax.all_gather(attention_normed_input, 'tensor', axis=0, tiled=True)  80.5 us
    reduce_scatter x1, waiting for transfers between devices, local(): lax.psum_scatter(times_transpose(d_projected, back_qkv).astype(jnp.bfloat...  77.3 us
    reduce_scatter x1, waiting for transfers between devices, local(): lax.psum_scatter(jnp.dot(activation, full_set[10], preferred_element_type...  76.9 us
    reduce_scatter x1, waiting for transfers between devices, local(): lax.psum_scatter((times_transpose(d_gate, back_set[8]) + times_transpose(...  65.7 us
    reduce_scatter x1, waiting for transfers between devices, local(): lax.psum_scatter(grad_down.astype(jnp.bfloat16), 'dp', scatter_dimension=...  62.9 us
    reduce_scatter x1, waiting for transfers between devices, local(): lax.psum_scatter(jnp.dot(context, full_set[6], preferred_element_type=jnp...  62 us
    all_gather x1, waiting for transfers between devices, local(): d_branch_all = lax.all_gather(d_branch, 'tensor', axis=0, tiled=True)  49.4 us
    dot_general x5, matrix products, contract_rows(): lax.dot_general(left, right, (((0,), (0,)), ((), ())), preferred_element_...  47.3 us
  transfers between devices with their start and end apart: 24, of which 19 were waited for; matrix products, arithmetic and copies ran while one was open for 18% of the time, Pallas kernels for 0%

profile of v1, /device:TPU:0, one launch (start us, length us, event | category | flops | bytes accessed | tf_op | source)
XLA Modules:
  0.0 1356.8 jit_solution(16355960102758444378)
XLA Ops:
  31.5 13.4 all-reduce.8
  51.1 15.1 %all-gather.17.cloned.1.call-done = bf16[2048,256]{1,0:T(8,128)(2,1)} async-done(((bf16[256,256]{1,0:T(8,128)(2,1)}), bf16[2048,256]{1,0:T(8,128)(2,1)}) %all-gather.17.cloned.1.call-update) | async-done | bytes 1048592 | tf_op jit(solution)/shard_map/all_gather | solution.py:156
  68.5 23.1 %all-gather.19.cloned.1.call-done = bf16[2048,256]{1,0:T(8,128)(2,1)} async-done(((bf16[256,256]{1,0:T(8,128)(2,1)}), bf16[2048,256]{1,0:T(8,128)(2,1)}) %all-gather.19.cloned.1.call-update) | async-done | bytes 1048592 | tf_op jit(solution)/shard_map/all_gather | solution.py:157
  93.9 80.5 %all-gather.13.cloned.1.call-done = bf16[1024,2048]{1,0:T(8,128)(2,1)} async-done(((bf16[256,2048]{1,0:T(8,128)(2,1)}), bf16[1024,2048]{1,0:T(8,128)(2,1)}) %all-gather.13.cloned.1.call-update) | async-done | bytes 4194320 | tf_op jit(solution)/shard_map/all_gather | solution.py:172
  206.1 16.8 %while.28 = (s32[]{:T(128)}, bf16[2,1024,2,128]{1,3,2,0:T(8,128)(2,1)}, f32[2,2,1024]{2,1,0:T(2,128)S(1)}, bf16[2,1024,128]{1,2,0:T(8,128)(2,1)S(1)}, bf16[2,102...) while((s32[]{:T(128)}, ...), condition=%wide.region_8.9_spmd.clone, body=%wide.region_5.8_spmd.clone.sunk | while | flops 1102313472 | bytes 31004760 | solution.py:190
  243.1 62.0 %reduce-scatter.12.cloned.1.call-done = bf16[256,2048]{1,0:T(8,128)(2,1)} async-done(((bf16[1024,2048]{1,0:T(8,128)(2,1)}), bf16[256,2048]{1,0:T(8,128)(2,1)}) %reduce-scatter.12.cloned.1.call-update) | async-done | bytes 1048592 | tf_op jit(solution)/shard_map/reduce_scatter | solution.py:195
  315.3 43.0 %collective-permute-done = bf16[256,2048]{1,0:T(8,128)(2,1)} collective-permute-done((bf16[256,2048]{1,0:T(8,128)(2,1)}, bf16[256,2048]{1,0:T(8,128)(2,1)}, u32[]{:S(2)}, u32[]{:S(2)}) %collective-permute-start) | collective-permute-done | bytes 1048608 | tf_op jit(solution)/shard_map/ppermute | solution.py:19
  358.3 43.4 %collective-permute-start.2 = (bf16[256,2048]{1,0:T(8,128)(2,1)}, bf16[256,2048]{1,0:T(8,128)(2,1)}, u32[]{:S(2)}, u32[]{:S(2)}) collective-permute-start(bf16[256,2048]{1,0:T(8,128)(2,1)} %collective-permute-done), channel_id=1, source_target_pairs={{0,1},{1,2},{2,3},{3,0},{4,5},{5,6},{6,7},{7,4},{8,9},{9,10},{10,1... | collective-permute-start | bytes 3145736 | tf_op jit(solution)/shard_map/ppermute | solution.py:19
  401.7 49.4 %all-gather.29.cloned.1.call-done = bf16[1024,2048]{1,0:T(8,128)(2,1)} async-done(((bf16[256,2048]{1,0:T(8,128)(2,1)}), bf16[1024,2048]{1,0:T(8,128)(2,1)}) %all-gather.29.cloned.1.call-update) | async-done | bytes 4194320 | tf_op jit(solution)/shard_map/all_gather | solution.py:231
  451.0 47.0 %all-gather.27.cloned.1.call-done = bf16[1536,2048]{1,0:T(8,128)(2,1)} async-done(((bf16[1536,256]{1,0:T(8,128)(2,1)}), bf16[1536,2048]{1,0:T(8,128)(2,1)}) %all-gather.27.cloned.1.call-update) | async-done | bytes 6291472 | tf_op jit(solution)/shard_map/all_gather | solution.py:164
  498.0 12.0 fusion.114
  517.0 28.7 %all-gather.25.cloned.1.call-done = bf16[2048,1536]{1,0:T(8,128)(2,1)} async-done(((bf16[256,1536]{1,0:T(8,128)(2,1)}), bf16[2048,1536]{1,0:T(8,128)(2,1)}) %all-gather.25.cloned.1.call-update) | async-done | bytes 6291472 | tf_op jit(solution)/shard_map/all_gather | solution.py:163
  545.6 11.8 fusion.113
  557.5 35.6 %all-gather.23.cloned.1.call-done = bf16[2048,1536]{1,0:T(8,128)(2,1)} async-done(((bf16[256,1536]{1,0:T(8,128)(2,1)}), bf16[2048,1536]{1,0:T(8,128)(2,1)}) %all-gather.23.cloned.1.call-update) | async-done | bytes 6291472 | tf_op jit(solution)/shard_map/all_gather | solution.py:162
  593.1 16.3 %multiply_convert_fusion = (bf16[1024,1536]{1,0:T(8,128)(2,1)S(1)}, bf16[1024,1536]{1,0:T(8,128)(2,1)S(1)}, bf16[1024,1536]{1,0:T(8,128)(2,1)}) fusion(f32[1024,1536]{1,0:T(8,128)} %fusion.114, f32[1024,1536]{1,0:T(8,128)} %fusion.113, bf16[1024,2048]{1,0:T(8,128)(2,1)} %constant_dynamic-update-slice_fusion.3, ...), kind=kOutput, calls=%fused_computation.75 | convolution fusion | flops 6467616768 | bytes 32505856 | tf_op jit(solution)/shard_map/dot_general | solution.py:204
  629.1 11.1 convolution_convert_fusion.3
  640.3 65.7 %reduce-scatter.16.cloned.1.call-done = bf16[256,2048]{1,0:T(8,128)(2,1)} async-done(((bf16[1024,2048]{1,0:T(8,128)(2,1)}), bf16[256,2048]{1,0:T(8,128)(2,1)}) %reduce-scatter.16.cloned.1.call-update) | async-done | bytes 1048592 | tf_op jit(solution)/shard_map/reduce_scatter | solution.py:240
  708.5 76.9 %reduce-scatter.14.cloned.1.call-done = bf16[256,2048]{1,0:T(8,128)(2,1)} async-done(((bf16[1024,2048]{1,0:T(8,128)(2,1)}), bf16[256,2048]{1,0:T(8,128)(2,1)}) %reduce-scatter.14.cloned.1.call-update) | async-done | bytes 1048592 | tf_op jit(solution)/shard_map/reduce_scatter | solution.py:208
  790.5 11.5 convolution_convert_fusion.1
  802.1 11.9 convolution_convert_fusion.2
  817.3 11.3 convolution_convert_fusion
  828.8 43.1 %all-gather.31.cloned.1.call-done = bf16[1024,2048]{1,0:T(8,128)(2,1)} async-done(((bf16[256,2048]{1,0:T(8,128)(2,1)}), bf16[1024,2048]{1,0:T(8,128)(2,1)}) %all-gather.31.cloned.1.call-update) | async-done | bytes 4194320 | tf_op jit(solution)/shard_map/all_gather | solution.py:251
  880.5 27.4 %while.29 = (s32[]{:T(128)}, f32[2,1024,2,128]{1,3,2,0:T(8,128)}, f32[2,1024,128]{2,1,0:T(8,128)}, bf16[2,1024,128]{2,1,0:T(8,128)(2,1)}, bf16[2,1024,128]{2,1,0...) while((s32[]{:T(128)}, f32[2,1024,2,128]{1,3,2,0:T(8,128)}, ...), condition=%wide.region_16.17_spmd.clone, body=%wide.region_14.16_spmd.clone.sunk | while | flops 2719348736 | bytes 101516552 | solution.py:257
  953.5 47.3 %reduce-scatter.28.cloned.1.call-done = bf16[256,1536]{1,0:T(8,128)(2,1)} async-done(((bf16[2048,1536]{1,0:T(8,128)(2,1)}), bf16[256,1536]{1,0:T(8,128)(2,1)}) %reduce-scatter.28.cloned.1.call-update) | async-done | bytes 786448 | tf_op jit(solution)/shard_map/reduce_scatter | solution.py:317
  1003.3 62.9 %reduce-scatter.32.cloned.1.call-done = bf16[1536,256]{1,0:T(8,128)(2,1)} async-done(((bf16[1536,2048]{1,0:T(8,128)(2,1)}), bf16[1536,256]{1,0:T(8,128)(2,1)}) %reduce-scatter.32.cloned.1.call-update) | async-done | bytes 786448 | tf_op jit(solution)/shard_map/reduce_scatter | solution.py:323
  1068.6 36.7 %reduce-scatter.22.cloned.1.call-done = bf16[256,256]{1,0:T(8,128)(2,1)} async-done(((bf16[2048,256]{1,0:T(8,128)(2,1)}), bf16[256,256]{1,0:T(8,128)(2,1)}) %reduce-scatter.22.cloned.1.call-update) | async-done | bytes 131088 | tf_op jit(solution)/shard_map/reduce_scatter | solution.py:299
  1106.9 38.0 %reduce-scatter.24.cloned.1.call-done = bf16[256,256]{1,0:T(8,128)(2,1)} async-done(((bf16[2048,256]{1,0:T(8,128)(2,1)}), bf16[256,256]{1,0:T(8,128)(2,1)}) %reduce-scatter.24.cloned.1.call-update) | async-done | bytes 131088 | tf_op jit(solution)/shard_map/reduce_scatter | solution.py:302
  1146.6 42.9 %reduce-scatter.26.cloned.1.call-done = bf16[512,256]{1,0:T(8,128)(2,1)} async-done(((bf16[512,2048]{1,0:T(8,128)(2,1)}), bf16[512,256]{1,0:T(8,128)(2,1)}) %reduce-scatter.26.cloned.1.call-update) | async-done | bytes 262160 | tf_op jit(solution)/shard_map/reduce_scatter | solution.py:311
  1191.2 43.0 %reduce-scatter.20.cloned.1.call-done = bf16[256,512]{1,0:T(8,128)(2,1)} async-done(((bf16[2048,512]{1,0:T(8,128)(2,1)}), bf16[256,512]{1,0:T(8,128)(2,1)}) %reduce-scatter.20.cloned.1.call-update) | async-done | bytes 262160 | tf_op jit(solution)/shard_map/reduce_scatter | solution.py:296
  1236.0 77.3 %reduce-scatter.18.cloned.1.call-done = bf16[256,2048]{1,0:T(8,128)(2,1)} async-done(((bf16[1024,2048]{1,0:T(8,128)(2,1)}), bf16[256,2048]{1,0:T(8,128)(2,1)}) %reduce-scatter.18.cloned.1.call-update) | async-done | bytes 1048592 | tf_op jit(solution)/shard_map/reduce_scatter | solution.py:280
  1315.2 18.2 %all-reduce.6 = (bf16[2048]{0:T(1024)(128)(2,1)S(1)}, bf16[128]{0:T(256)(128)(2,1)S(1)}, bf16[128]{0:T(256)(128)(2,1)S(1)}, bf16[2048]{0:T(1024)(128)(2,1)S(1)}) all-reduce(f32[2048]{0:T(1024)S(1)} %get-tuple-element.175, f32[128]{0:T(128)S(1)} %bitcast_reduce_fusion, ...), channel_id=1, replica_groups=mesh['dp'=8,'tensor'=4] {'tensor'}, use_global_device_ids=true, to_apply=%region_22.23 | all-reduce | flops 4352 | bytes 26112 | tf_op jit(solution)/shard_map/psum | solution.py:290
  1333.4 12.3 all-reduce.7
  (306 shorter events, 247.4 us)
Async XLA Ops:
  7.2 40.7 %all-gather.15.cloned.1.call-start = ((), (), s32[]{:S(2)}) async-start(), calls=%async_computation.12 | async-start | bytes 2359296 | tf_op jit(solution)/shard_map/all_gather | solution.py:155
  8.0 58.2 %all-gather.17.cloned.1.call-start = ((), (), s32[]{:S(2)}) async-start(), calls=%async_computation.13 | async-start | bytes 1179648 | tf_op jit(solution)/shard_map/all_gather | solution.py:156
  8.7 82.8 %all-gather.19.cloned.1.call-start = ((), (), s32[]{:S(2)}) async-start(), calls=%async_computation.14 | async-start | bytes 1179648 | tf_op jit(solution)/shard_map/all_gather | solution.py:157
  9.5 164.9 %all-gather.13.cloned.1.call-start = ((), (), s32[]{:S(2)}) async-start(), calls=%async_computation.11 | async-start | bytes 5242880 | tf_op jit(solution)/shard_map/all_gather | solution.py:172
  25.7 197.2 %all-gather.21.cloned.1.call-start = ((), (), s32[]{:S(2)}) async-start(), calls=%async_computation.15 | async-start | bytes 2359296 | tf_op jit(solution)/shard_map/all_gather | solution.py:160
  26.3 278.9 %reduce-scatter.12.cloned.1.call-start = ((), (), s32[]{:S(2)}) async-start(), calls=%async_computation.16 | async-start | bytes 5242880 | tf_op jit(solution)/shard_map/reduce_scatter | solution.py:195
  44.9 155.3 %copy-start.45 = (f32[128]{0:T(128)}, f32[128]{0:T(128)S(1)}, u32[]{:S(2)}) copy-start(f32[128]{0:T(128)S(1)} %convert_element_type.188) | copy-start | bytes 1540
  48.0 155.0 %copy-start.43 = (f32[128]{0:T(128)}, f32[128]{0:T(128)S(1)}, u32[]{:S(2)}) copy-start(f32[128]{0:T(128)S(1)} %convert_element_type.191) | copy-start | bytes 1540
  229.7 221.4 %all-gather.29.cloned.1.call-start = ((), (), s32[]{:S(2)}) async-start(), calls=%async_computation.21 | async-start | bytes 5242880 | tf_op jit(solution)/shard_map/all_gather | solution.py:231
  232.1 265.9 %all-gather.27.cloned.1.call-start = ((), (), s32[]{:S(2)}) async-start(), calls=%async_computation.19 | async-start | bytes 7077888 | tf_op jit(solution)/shard_map/all_gather | solution.py:164
  232.8 312.8 %all-gather.25.cloned.1.call-start = ((), (), s32[]{:S(2)}) async-start(), calls=%async_computation.18 | async-start | bytes 7077888 | tf_op jit(solution)/shard_map/all_gather | solution.py:163
  233.6 359.5 %all-gather.23.cloned.1.call-start = ((), (), s32[]{:S(2)}) async-start(), calls=%async_computation.17 | async-start | bytes 7077888 | tf_op jit(solution)/shard_map/all_gather | solution.py:162
  234.2 471.8 %reduce-scatter.16.cloned.1.call-start = ((), (), s32[]{:S(2)}) async-start(), calls=%async_computation.22 | async-start | bytes 5242880 | tf_op jit(solution)/shard_map/reduce_scatter | solution.py:240
  311.4 46.9 %collective-permute-start = (bf16[256,2048]{1,0:T(8,128)(2,1)}, bf16[256,2048]{1,0:T(8,128)(2,1)}, u32[]{:S(2)}, u32[]{:S(2)}) collective-permute-start(bf16[256,2048]{1,0:T(8,128)(2,1)} %get-tuple-element.225), channel_id=1, source_target_pairs={{0,1},{1,2},{2,3},{3,0},{4,5},{5,6},{6,7},{7,4},{8,9},{9,10},{10,1... | collective-permute-start | bytes 3145736 | tf_op jit(solution)/shard_map/ppermute | solution.py:19
  312.8 199.5 %collective-permute-start.1 = (bf16[256,2048]{1,0:T(8,128)(2,1)}, bf16[256,2048]{1,0:T(8,128)(2,1)}, u32[]{:S(2)}, u32[]{:S(2)}) collective-permute-start(bf16[256,2048]{1,0:T(8,128)(2,1)} %get-tuple-element.225), channel_id=1, source_target_pairs={{0,3},{1,0},{2,1},{3,2},{4,7},{5,4},{6,5},{7,6},{8,11},{9,8},{10,9... | collective-permute-start | bytes 3145736 | tf_op jit(solution)/shard_map/ppermute | solution.py:22
  358.3 156.3 %collective-permute-start.2 = (bf16[256,2048]{1,0:T(8,128)(2,1)}, bf16[256,2048]{1,0:T(8,128)(2,1)}, u32[]{:S(2)}, u32[]{:S(2)}) collective-permute-start(bf16[256,2048]{1,0:T(8,128)(2,1)} %collective-permute-done), channel_id=1, source_target_pairs={{0,1},{1,2},{2,3},{3,0},{4,5},{5,6},{6,7},{7,4},{8,9},{9,10},{10,1... | collective-permute-start | bytes 3145736 | tf_op jit(solution)/shard_map/ppermute | solution.py:19
  629.0 156.4 %reduce-scatter.14.cloned.1.call-start = ((), (), s32[]{:S(2)}) async-start(), calls=%async_computation.20 | async-start | bytes 5242880 | tf_op jit(solution)/shard_map/reduce_scatter | solution.py:208
  640.2 231.7 %all-gather.31.cloned.1.call-start = ((), (), s32[]{:S(2)}) async-start(), calls=%async_computation.23 | async-start | bytes 5242880 | tf_op jit(solution)/shard_map/all_gather | solution.py:251
  790.5 160.4 %reduce-scatter.30.cloned.1.call-start = ((), (), s32[]{:S(2)}) async-start(), calls=%async_computation.30 | async-start | bytes 7077888 | tf_op jit(solution)/shard_map/reduce_scatter | solution.py:320
  802.0 198.8 %reduce-scatter.28.cloned.1.call-start = ((), (), s32[]{:S(2)}) async-start(), calls=%async_computation.29 | async-start | bytes 7077888 | tf_op jit(solution)/shard_map/reduce_scatter | solution.py:317
  814.1 252.1 %reduce-scatter.32.cloned.1.call-start = ((), (), s32[]{:S(2)}) async-start(), calls=%async_computation.31 | async-start | bytes 7077888 | tf_op jit(solution)/shard_map/reduce_scatter | solution.py:323
  828.7 276.6 %reduce-scatter.22.cloned.1.call-start = ((), (), s32[]{:S(2)}) async-start(), calls=%async_computation.26 | async-start | bytes 1179648 | tf_op jit(solution)/shard_map/reduce_scatter | solution.py:299
  930.9 214.1 %reduce-scatter.24.cloned.1.call-start = ((), (), s32[]{:S(2)}) async-start(), calls=%async_computation.27 | async-start | bytes 1179648 | tf_op jit(solution)/shard_map/reduce_scatter | solution.py:302
  931.4 258.0 %reduce-scatter.26.cloned.1.call-start = ((), (), s32[]{:S(2)}) async-start(), calls=%async_computation.28 | async-start | bytes 2359296 | tf_op jit(solution)/shard_map/reduce_scatter | solution.py:311
  937.8 296.4 %reduce-scatter.20.cloned.1.call-start = ((), (), s32[]{:S(2)}) async-start(), calls=%async_computation.25 | async-start | bytes 2359296 | tf_op jit(solution)/shard_map/reduce_scatter | solution.py:296
  941.0 372.3 %reduce-scatter.18.cloned.1.call-start = ((), (), s32[]{:S(2)}) async-start(), calls=%async_computation.24 | async-start | bytes 5242880 | tf_op jit(solution)/shard_map/reduce_scatter | solution.py:280
  950.8 362.5 %copy-start.1 = (bf16[256,2048]{1,0:T(8,128)(2,1)S(1)}, bf16[256,2048]{1,0:T(8,128)(2,1)}, u32[]{:S(2)}) copy-start(bf16[256,2048]{1,0:T(8,128)(2,1)} %param.19) | copy-start | bytes 3145732
  950.8 362.5 %copy-start.37 = (f32[8,1,256]{2,1,0:T(1,128)S(1)}, f32[8,1,256]{2,1,0:T(1,128)}, u32[]{:S(2)}) copy-start(f32[8,1,256]{2,1,0:T(1,128)} %copy-done.36) | copy-start | bytes 24580
  950.8 362.5 %copy-start.42 = (f32[256]{0:T(256)S(1)}, f32[256]{0:T(256)}, u32[]{:S(2)}) copy-start(f32[256]{0:T(256)} %copy-done.41) | copy-start | bytes 3076
  953.5 361.7 %copy-start.40 = (f32[2048]{0:T(1024)S(1)}, f32[2048]{0:T(1024)}, u32[]{:S(2)}) copy-start(f32[2048]{0:T(1024)} %get-tuple-element.171) | copy-start | bytes 24580
  953.5 393.4 %copy-start.17 = (f32[256,2048]{1,0:T(8,128)S(1)}, f32[256,2048]{1,0:T(8,128)}, u32[]{:S(2)}) copy-start(f32[256,2048]{1,0:T(8,128)} %get-tuple-element.223) | copy-start | bytes 6291460
  953.5 393.4 %copy-start.47 = (f32[256]{0:T(256)S(1)}, f32[256]{0:T(256)}, u32[]{:S(2)}) copy-start(f32[256]{0:T(256)} %get-tuple-element.254) | copy-start | bytes 3076
  (57 other events, 416.2 us)
Sparse Core Ops, SparseCore 0:
  10.0 30.6 all-gather.14
  42.5 23.5 all-gather.16
  68.0 23.4 all-gather.18
  93.6 80.7 all-gather.12
  176.1 26.7 all-gather.20
  229.8 75.3 reduce-scatter.11
  307.4 143.6 all-gather.28
  453.1 44.8 all-gather.26
  500.1 45.5 all-gather.24
  547.5 45.5 all-gather.22
  629.2 76.7 reduce-scatter.15
  708.1 77.2 reduce-scatter.13
  790.6 81.2 all-gather.30
  875.5 60.2 reduce-scatter.29
  939.0 61.7 reduce-scatter.27
  1004.4 61.7 reduce-scatter.31
  1069.2 36.0 reduce-scatter.21
  1108.9 36.0 reduce-scatter.23
  1148.2 41.2 reduce-scatter.25
  1193.0 41.2 reduce-scatter.19
  1236.5 76.7 reduce-scatter.17
